TPU v7x, 128 devices: a whole 4x4x4 slice. The times are simulated.
128 devices in a mesh: leaf: 4 (over y), row: 4 (over z), col: 8 (over x, core).
Axes of the slice: x: 4, y: 4, z: 4, core: 2. Of those that a mesh axis runs over, the one named last changes fastest.
Arguments:
- rhs_leaf: bfloat16 [4, 12288, 256], P('leaf', 'col'), may hold values from -6 to 6
- rhs_parent: bfloat16 [16384, 256], P(('leaf', 'row', 'col')), may hold values from -6 to 6
- inv_leaf: bfloat16 [4, 12288, 12288], P('leaf', 'row', 'col'), as said below
- panel: bfloat16 [4, 6144, 12288], P('leaf', 'col', 'row'), may hold values from -0.0546875 to 0.0546875
- row_map: int32 [4, 6144], P('leaf', 'col'), may hold values from 0 to 16383, as said below
- inv_parent: bfloat16 [16384, 16384], P(('row', 'col'), 'leaf'), as said below
Outputs:
- sol_leaf: bfloat16 [4, 12288, 256], P('leaf', 'col')
- sol_parent: bfloat16 [16384, 256], P(('leaf', 'row', 'col'))
Inputs may be any that keep to these rules, and one draw needn't show every extreme that they name: Within one leaf the 6144 entries of row_map are distinct parent rows. Split the parent rows into 128 owner blocks of 16384 // 128 consecutive rows: in each aligned block of 192 consecutive entries of a leaf, at most 2 entries fall in one owner block, and exactly 2 in some. `inv_leaf`: lower triangular: zeros above the diagonal, diagonal entries between 0.5 and 2. `inv_parent`: lower triangular: zeros above the diagonal, diagonal entries between 0.5 and 2.
All inputs are finite; a program needn't handle non-finite values.
Results may differ from a plain program's by a relative error of at most 0.01.
Values may be sent and summed in bfloat16 or wider, within the bound.
A program may use at most 128 MiB of HBM per device.

v0:
```python
import jax
import jax.numpy as jnp
from jax import lax
from jax.sharding import PartitionSpec as P


def dense_updates(update, row_map, rhs_parent):
    total_rows = rhs_parent.shape[0] * lax.axis_size(("leaf", "row", "col"))
    dense = jnp.zeros((total_rows, rhs_parent.shape[1]), jnp.float32)
    dense = dense.at[row_map[0]].add(-update)
    offset = lax.axis_index(("leaf", "row", "col")) * rhs_parent.shape[0]
    own_rows = lax.dynamic_slice_in_dim(dense, offset, rhs_parent.shape[0], 0) + rhs_parent.astype(
        jnp.float32
    )
    return lax.dynamic_update_slice_in_dim(dense, own_rows, offset, 0)


def per_device(rhs_leaf, rhs_parent, inv_leaf, panel, row_map, inv_parent):
    leaf_part = jnp.dot(inv_leaf[0], rhs_leaf[0], preferred_element_type=jnp.float32)
    forward = lax.psum(leaf_part, "col").astype(jnp.bfloat16)
    update = jnp.dot(panel[0], forward, preferred_element_type=jnp.float32)
    dense = dense_updates(update, row_map, rhs_parent)
    leaf_block = lax.psum_scatter(dense, "leaf", scatter_dimension=0, tiled=True)
    reduced = lax.psum(leaf_block, ("row", "col")).astype(jnp.bfloat16)
    parent_part = jnp.dot(inv_parent, reduced, preferred_element_type=jnp.float32)
    fwd_parent = lax.psum(parent_part, "leaf").astype(jnp.bfloat16)
    back_part = lax.dot_general(
        inv_parent, fwd_parent, (((0,), (0,)), ((), ())), preferred_element_type=jnp.float32
    )
    sol_parent = lax.psum_scatter(
        back_part, ("row", "col"), scatter_dimension=0, tiled=True
    ).astype(jnp.bfloat16)
    whole_parent = lax.all_gather(sol_parent, ("leaf", "row", "col"), axis=0, tiled=True)
    picked = jnp.take(whole_parent, row_map[0], axis=0)
    coupling_part = lax.dot_general(
        panel[0], picked, (((0,), (0,)), ((), ())), preferred_element_type=jnp.float32
    )
    coupling = lax.psum(coupling_part, "col")
    corrected = (forward.astype(jnp.float32) - coupling).astype(jnp.bfloat16)
    final_part = lax.dot_general(
        inv_leaf[0], corrected, (((0,), (0,)), ((), ())), preferred_element_type=jnp.float32
    )
    sol_leaf = lax.psum(final_part, "row").astype(jnp.bfloat16)
    return (sol_leaf[None], sol_parent)


def solution(mesh):
    in_specs = (
        P("leaf", "col", None),
        P(("leaf", "row", "col"), None),
        P("leaf", "row", "col"),
        P("leaf", "col", "row"),
        P("leaf", "col"),
        P(("row", "col"), "leaf"),
    )
    out_specs = (P("leaf", "col", None), P(("leaf", "row", "col"), None))
    return jax.shard_map(
        per_device, mesh=mesh, in_specs=in_specs, out_specs=out_specs, check_vma=False
    )
```

profile of v0, /device:TPU:0, one launch (start us, length us, event | category | flops | bytes accessed | tf_op | source)
XLA Modules:
  0.0 728.7 jit_solution(5863380692495050478)
XLA Ops:
  7.2 1.1 copy-done
  8.3 8.0 %fusion.2 = f32[3072,256]{1,0:T(8,128)} fusion(bf16[1,3072,1536]{2,1,0:T(8,128)(2,1)} %param.8, bf16[1,1536,256]{2,1,0:T(8,128)(2,1)S(1)} %copy-done), kind=kOutput, calls=%fused_computation.4 | convolution fusion | flops 2415919104 | bytes 13369344 | tf_op jit(solution)/shard_map/dot_general | solution.py:19
  16.3 56.8 %all-reduce.7 = bf16[3072,256]{1,0:T(8,128)(2,1)S(1)} all-reduce(f32[3072,256]{1,0:T(8,128)} %fusion.2), channel_id=1, replica_groups=mesh['leaf'=4,'row'=4,'col'=8] {'col'}, use_global_device_ids=true, to_apply=%region_0.0 | all-reduce | flops 786432 | bytes 4718592 | tf_op jit(solution)/shard_map/psum | solution.py:20
  73.1 3.8 fusion.21
  76.9 0.3 copy.12
  77.2 12.3 %scatter_custom_fusion = f32[16384,256]{1,0:T(8,128)} fusion(s32[768]{0:T(1024)S(1)} %fusion.34, f32[768,256]{1,0:T(8,128)S(1)} %copy.12, f32[]{:T(128)} %constant.14.clone.1), kind=kCustom, calls=%fused_computation.6 | custom fusion | flops 196608 | bytes 16777220 | tf_op jit(solution)/shard_map/scatter-add | solution.py:10
  89.5 1.6 add_dynamic-update-slice_fusion
  91.0 0.0 reduce-scatter.5.cloned.1.call-start
  91.1 148.2 %reduce-scatter.3.cloned.1.call-done = f32[4096,256]{1,0:T(8,128)} async-done(((f32[16384,256]{1,0:T(8,128)}), f32[4096,256]{1,0:T(8,128)}) %reduce-scatter.3.cloned.1.call-update) | async-done | bytes 4194320 | tf_op jit(solution)/shard_map/reduce_scatter | solution.py:23
  239.3 153.3 %all-reduce.8 = bf16[4096,256]{1,0:T(8,128)(2,1)} all-reduce(f32[4096,256]{1,0:T(8,128)} %reduce-scatter.3.cloned.1.call-done), channel_id=1, replica_groups=mesh['leaf'=4,'row'=4,'col'=8] {'row','col'}, use_global_device_ids=true, to_apply=%region_3.0 | all-reduce | flops 1048576 | bytes 6291456 | tf_op jit(solution)/shard_map/psum | solution.py:24
  392.6 4.1 fusion.24
  396.8 20.8 %all-reduce.9 = bf16[512,256]{0,1:T(8,128)(2,1)S(1)} all-reduce(f32[512,256]{0,1:T(8,128)S(1)} %fusion.24), channel_id=1, replica_groups=mesh['leaf'=4,'row'=4,'col'=8] {'leaf'}, use_global_device_ids=true, to_apply=%region_4.0 | all-reduce | flops 131072 | bytes 786432 | tf_op jit(solution)/shard_map/psum | solution.py:26
  417.6 5.4 convolution_bitcast_fusion
  423.1 76.9 %reduce-scatter.5.cloned.1.call-done = f32[128,256]{0,1:T(8,128)} async-done(((f32[4096,256]{0,1:T(8,128)}), f32[128,256]{0,1:T(8,128)}) %reduce-scatter.5.cloned.1.call-update) | async-done | bytes 131088 | tf_op jit(solution)/shard_map/reduce_scatter | solution.py:30
  500.0 1.5 convert_element_type.29
  501.6 80.3 %all-gather.2.cloned.1.call-done = bf16[16384,256]{0,1:T(8,128)(2,1)} async-done(((bf16[128,256]{0,1:T(8,128)(2,1)}), bf16[16384,256]{0,1:T(8,128)(2,1)}) %all-gather.2.cloned.1.call-update) | async-done | bytes 8388624 | tf_op jit(solution)/shard_map/all_gather | solution.py:33
  581.9 11.9 %copy.13 = bf16[16384,256]{1,0:T(8,128)(2,1)} copy(bf16[16384,256]{0,1:T(8,128)(2,1)} %all-gather.2.cloned.1.call-done) | data formatting | bytes 16777216 | tf_op jit(solution)/shard_map/all_gather | solution.py:33
  593.8 6.6 gather_fusion
  600.3 6.1 fusion.10
  606.5 0.7 copy.15
  607.3 68.0 %all-reduce.6.cloned.1.call-done = f32[3072,256]{1,0:T(8,128)} async-done(((f32[3072,256]{1,0:T(8,128)}), f32[3072,256]{1,0:T(8,128)}) %all-reduce.6.cloned.1.call-update) | async-done | bytes 3145744 | tf_op jit(solution)/shard_map/psum | solution.py:38
  675.3 8.5 %fusion.13 = f32[1536,256]{0,1:T(8,128)} fusion(bf16[1,3072,1536]{2,1,0:T(8,128)(2,1)} %param.8, f32[3072,256]{1,0:T(8,128)} %all-reduce.6.cloned.1.call-done, bf16[3072,256]{1,0:T(8,128)(2,1)S(1)} %all-reduce.7), kind=kOutput, calls=%fused_computation.15 | convolution fusion | flops 2418278400 | bytes 15728640 | tf_op jit(solution)/shard_map/dot_general | solution.py:40
  683.7 37.3 %all-reduce.10 = bf16[1536,256]{0,1:T(8,128)(2,1)S(1)} all-reduce(f32[1536,256]{0,1:T(8,128)} %fusion.13), channel_id=1, replica_groups=mesh['leaf'=4,'row'=4,'col'=8] {'row'}, use_global_device_ids=true, to_apply=%region_7.8 | all-reduce | flops 393216 | bytes 2359296 | tf_op jit(solution)/shard_map/psum | solution.py:43
  721.0 1.2 copy.14
  (20 shorter events, 0.3 us)
Async XLA Ops:
  7.2 1.1 copy-start
  7.2 232.2 %reduce-scatter.3.cloned.1.call-start = ((), (), s32[]{:S(2)}) async-start(), calls=%async_computation.2 | async-start | bytes 20971520 | tf_op jit(solution)/shard_map/reduce_scatter | solution.py:23
  73.1 4.1 copy-start.4
  77.2 12.3 %copy-start.3 = (bf16[128,256]{1,0:T(8,128)(2,1)S(1)}, bf16[128,256]{1,0:T(8,128)(2,1)}, u32[]{:S(2)}) copy-start(bf16[128,256]{1,0:T(8,128)(2,1)} %param.7) | copy-start | bytes 196612
  91.0 408.9 %reduce-scatter.5.cloned.1.call-start = ((), (), s32[]{:S(2)}) async-start(), calls=%async_computation.3 | async-start | bytes 4325376 | tf_op jit(solution)/shard_map/reduce_scatter | solution.py:30
  423.0 158.9 %all-gather.2.cloned.1.call-start = ((), (), s32[]{:S(2)}) async-start(), calls=%async_computation.4 | async-start | bytes 8454144 | tf_op jit(solution)/shard_map/all_gather | solution.py:33
  501.5 173.7 %all-reduce.6.cloned.1.call-start = ((), (), s32[]{:S(2)}) async-start(), calls=%async_computation.5 | async-start | bytes 6291456 | tf_op jit(solution)/shard_map/psum | solution.py:38
  600.3 6.2 copy-start.2
  675.3 46.9 %copy-start.1 = (bf16[1,1536,256]{2,1,0:T(8,128)(2,1)S(1)}, bf16[1,1536,256]{2,1,0:T(8,128)(2,1)}, u32[]{:S(2)}) copy-start(bf16[1,1536,256]{2,1,0:T(8,128)(2,1)} %param.6) | copy-start | bytes 2359300
Sparse Core Ops, SparseCore 0:
  91.2 148.1 reduce-scatter.2
  423.1 76.8 reduce-scatter.4
  503.4 78.4 all-gather.1
  606.6 68.5 all-reduce.5
where the time goes:
time: 729 us
  waiting for transfers between devices  374 us (51%)
  blocking collectives  268 us (37%)
  matrix products  35.8 us (5%)
  local copies, waits for them, and re-layouts  21.7 us (3%)
  other arithmetic  15.4 us (2%)
  between operations  13.9 us (2%)
    psum x1, blocking collectives, per_device(): reduced = lax.psum(leaf_block, ('row', 'col')).astype(jnp.bfloat16)  153 us
    reduce_scatter x1, waiting for transfers between devices, per_device(): lax.psum_scatter(dense, 'leaf', scatter_dimension=0, tiled=True)  148 us
    all_gather x1, waiting for transfers between devices, per_device(): lax.all_gather(sol_parent, ('leaf', 'row', 'col'), axis=0, tiled=True)  80.3 us
    reduce_scatter x1, waiting for transfers between devices, per_device(): lax.psum_scatter(back_part, ('row', 'col'), scatter_dimension=0, tiled=True)  76.9 us
    psum x1, waiting for transfers between devices, per_device(): coupling = lax.psum(coupling_part, 'col')  68 us
    psum x1, blocking collectives, per_device(): forward = lax.psum(leaf_part, 'col').astype(jnp.bfloat16)  56.8 us
    psum x1, blocking collectives, per_device(): sol_leaf = lax.psum(final_part, 'row').astype(jnp.bfloat16)  37.3 us
    psum x1, blocking collectives, per_device(): fwd_parent = lax.psum(parent_part, 'leaf').astype(jnp.bfloat16)  20.8 us
  transfers between devices with their start and end apart: 4, of which 4 were waited for; matrix products, arithmetic and copies ran while one was open for 0% of the time, Pallas kernels for 0%

commit v1 on v0

--- a/solution.py
+++ b/solution.py
@@ -2,6 +2,15 @@
 import jax.numpy as jnp
 from jax import lax
 from jax.sharding import PartitionSpec as P
+
+
+def grid_find(vals, which_axis, d0):
+    seen = []
+    for _ in range(lax.axis_size(which_axis)):
+        seen.append(vals)
+    t1 = jnp.stack(seen)
+    upper = lax.all_to_all(t1, which_axis, split_axis=0, concat_axis=0)
+    return jnp.concatenate(upper, axis=d0)
 
 
 def dense_updates(update, row_map, rhs_parent):
@@ -30,7 +39,7 @@
     sol_parent = lax.psum_scatter(
         back_part, ("row", "col"), scatter_dimension=0, tiled=True
     ).astype(jnp.bfloat16)
-    whole_parent = lax.all_gather(sol_parent, ("leaf", "row", "col"), axis=0, tiled=True)
+    whole_parent = grid_find(sol_parent, ("leaf", "row", "col"), 0)
     picked = jnp.take(whole_parent, row_map[0], axis=0)
     coupling_part = lax.dot_general(
         panel[0], picked, (((0,), (0,)), ((), ())), preferred_element_type=jnp.float32

time: 729 us -> 754 us (1.034)
  waiting for transfers between devices: 374 us -> 399 us
  starting transfers between devices: 0.16 us -> 8.59 us
  local copies, waits for them, and re-layouts: 21.7 us -> 13.4 us
    all_to_all x0 -> x1, waiting for transfers between devices: none -> 101 us  [grid_find(): upper = lax.all_to_all(t1, which_axis, split_axis=0, concat_axis=0)]
    all_gather x1 -> x0, waiting for transfers between devices: 80.3 us -> none  [per_device(): lax.all_gather(sol_parent, ('leaf', 'row', 'col'), axis=0, tiled=True)]
    all_gather x1 -> x0, local copies, waits for them, and re-layouts: 11.9 us -> none  [per_device(): lax.all_gather(sol_parent, ('leaf', 'row', 'col'), axis=0, tiled=True)]
    all_to_all x0 -> x1, starting transfers between devices: none -> 8.46 us  [grid_find(): upper = lax.all_to_all(t1, which_axis, split_axis=0, concat_axis=0)]
where the time goes in v1:
time: 754 us; the launch traced here: 753 us
  waiting for transfers between devices  399 us (53%)
  blocking collectives  268 us (36%)
  matrix products  35.8 us (5%)
  other arithmetic  14.8 us (2%)
  between operations  13.9 us (2%)
  local copies, waits for them, and re-layouts  13.4 us (2%)
  starting transfers between devices  8.59 us (1%)
    psum x1, blocking collectives, per_device(): reduced = lax.psum(leaf_block, ('row', 'col')).astype(jnp.bfloat16)  153 us
    reduce_scatter x1, waiting for transfers between devices, per_device(): lax.psum_scatter(dense, 'leaf', scatter_dimension=0, tiled=True)  148 us
    all_to_all x1, waiting for transfers between devices, grid_find(): upper = lax.all_to_all(t1, which_axis, split_axis=0, concat_axis=0)  101 us
    reduce_scatter x1, waiting for transfers between devices, per_device(): lax.psum_scatter(back_part, ('row', 'col'), scatter_dimension=0, tiled=True)  77 us
    psum x1, waiting for transfers between devices, per_device(): coupling = lax.psum(coupling_part, 'col')  72.9 us
    psum x1, blocking collectives, per_device(): forward = lax.psum(leaf_part, 'col').astype(jnp.bfloat16)  56.8 us
    psum x1, blocking collectives, per_device(): sol_leaf = lax.psum(final_part, 'row').astype(jnp.bfloat16)  37.3 us
    psum x1, blocking collectives, per_device(): fwd_parent = lax.psum(parent_part, 'leaf').astype(jnp.bfloat16)  20.8 us
  transfers between devices with their start and end apart: 4, of which 4 were waited for; matrix products, arithmetic and copies ran while one was open for 0% of the time, Pallas kernels for 0%

profile of v1, /device:TPU:0, one launch (start us, length us, event | category | flops | bytes accessed | tf_op | source)
XLA Modules:
  0.0 753.4 jit_solution(13089499741149038127)
XLA Ops:
  7.2 1.1 copy-done
  8.3 8.0 %fusion.2 = f32[3072,256]{1,0:T(8,128)} fusion(bf16[1,3072,1536]{2,1,0:T(8,128)(2,1)} %param.8, bf16[1,1536,256]{2,1,0:T(8,128)(2,1)S(1)} %copy-done), kind=kOutput, calls=%fused_computation.4 | convolution fusion | flops 2415919104 | bytes 13369344 | tf_op jit(solution)/shard_map/dot_general | solution.py:28
  16.3 56.8 %all-reduce.7 = bf16[3072,256]{1,0:T(8,128)(2,1)S(1)} all-reduce(f32[3072,256]{1,0:T(8,128)} %fusion.2), channel_id=1, replica_groups=mesh['leaf'=4,'row'=4,'col'=8] {'col'}, use_global_device_ids=true, to_apply=%region_0.0 | all-reduce | flops 786432 | bytes 4718592 | tf_op jit(solution)/shard_map/psum | solution.py:29
  73.1 3.8 fusion.21
  76.9 0.3 copy.12
  77.2 12.3 %scatter_custom_fusion = f32[16384,256]{1,0:T(8,128)} fusion(s32[768]{0:T(1024)S(1)} %fusion.34, f32[768,256]{1,0:T(8,128)S(1)} %copy.12, f32[]{:T(128)} %constant.14.clone.1), kind=kCustom, calls=%fused_computation.6 | custom fusion | flops 196608 | bytes 16777220 | tf_op jit(solution)/shard_map/scatter-add | solution.py:19
  89.5 1.6 add_dynamic-update-slice_fusion
  91.1 148.2 %reduce-scatter.3.cloned.1.call-done = f32[4096,256]{1,0:T(8,128)} async-done(((f32[16384,256]{1,0:T(8,128)}), f32[4096,256]{1,0:T(8,128)}) %reduce-scatter.3.cloned.1.call-update) | async-done | bytes 4194320 | tf_op jit(solution)/shard_map/reduce_scatter | solution.py:32
  239.3 153.3 %all-reduce.8 = bf16[4096,256]{1,0:T(8,128)(2,1)} all-reduce(f32[4096,256]{1,0:T(8,128)} %reduce-scatter.3.cloned.1.call-done), channel_id=1, replica_groups=mesh['leaf'=4,'row'=4,'col'=8] {'row','col'}, use_global_device_ids=true, to_apply=%region_3.0 | all-reduce | flops 1048576 | bytes 6291456 | tf_op jit(solution)/shard_map/psum | solution.py:33
  392.6 4.1 fusion.24
  396.8 20.8 %all-reduce.9 = bf16[512,256]{0,1:T(8,128)(2,1)S(1)} all-reduce(f32[512,256]{0,1:T(8,128)S(1)} %fusion.24), channel_id=1, replica_groups=mesh['leaf'=4,'row'=4,'col'=8] {'leaf'}, use_global_device_ids=true, to_apply=%region_4.0 | all-reduce | flops 131072 | bytes 786432 | tf_op jit(solution)/shard_map/psum | solution.py:35
  417.6 5.4 convolution_bitcast_fusion
  423.0 77.0 %reduce-scatter.5.cloned.1.call-done = f32[128,256]{0,1:T(8,128)} async-done(((f32[4096,256]{0,1:T(8,128)}), f32[128,256]{0,1:T(8,128)}) %reduce-scatter.5.cloned.1.call-update) | async-done | bytes 131088 | tf_op jit(solution)/shard_map/reduce_scatter | solution.py:39
  500.0 0.9 convert_element_type.29
  500.9 0.1 copy.13
  501.0 4.3 stack.2
  505.3 8.5 %all-to-all-start = ((bf16[128,128,256]{2,1,0:T(8,128)(2,1)}), bf16[128,128,256]{2,1,0:T(8,128)(2,1)}, u32[]{:S(2)}, u32[]{:S(2)}) async-start(bf16[128,128,256]{2,1,0:T(8,128)(2,1)} %stack.2), calls=%async_computation.2 | async-start | bytes 16777216 | tf_op jit(solution)/shard_map/all_to_all | solution.py:12
  513.8 100.6 %all-to-all-done = bf16[128,128,256]{2,1,0:T(8,128)(2,1)} async-done(((bf16[128,128,256]{2,1,0:T(8,128)(2,1)}), bf16[128,128,256]{2,1,0:T(8,128)(2,1)}, u32[]{:S(2)}, u32[]{:S(2)}) %all-to-all-start) | async-done | bytes 8388640 | tf_op jit(solution)/shard_map/all_to_all | solution.py:12
  614.4 6.6 gather_fusion
  621.0 6.1 fusion.10
  627.1 72.9 %all-reduce.6.cloned.1.call-done = f32[3072,256]{1,0:T(8,128)} async-done(((f32[3072,256]{1,0:T(8,128)}), f32[3072,256]{1,0:T(8,128)}) %all-reduce.6.cloned.1.call-update) | async-done | bytes 3145744 | tf_op jit(solution)/shard_map/psum | solution.py:47
  700.0 8.5 %fusion.13 = f32[1536,256]{0,1:T(8,128)} fusion(bf16[1,3072,1536]{2,1,0:T(8,128)(2,1)} %param.8, f32[3072,256]{1,0:T(8,128)} %all-reduce.6.cloned.1.call-done, bf16[3072,256]{1,0:T(8,128)(2,1)S(1)} %all-reduce.7), kind=kOutput, calls=%fused_computation.15 | convolution fusion | flops 2418278400 | bytes 15728640 | tf_op jit(solution)/shard_map/dot_general | solution.py:49
  708.4 37.3 %all-reduce.10 = bf16[1536,256]{0,1:T(8,128)(2,1)S(1)} all-reduce(f32[1536,256]{0,1:T(8,128)} %fusion.13), channel_id=1, replica_groups=mesh['leaf'=4,'row'=4,'col'=8] {'row'}, use_global_device_ids=true, to_apply=%region_7.8 | all-reduce | flops 393216 | bytes 2359296 | tf_op jit(solution)/shard_map/psum | solution.py:52
  745.7 1.2 copy.14
  (19 shorter events, 0.2 us)
Async XLA Ops:
  7.2 1.1 copy-start
  7.2 232.2 %reduce-scatter.3.cloned.1.call-start = ((), (), s32[]{:S(2)}) async-start(), calls=%async_computation.3 | async-start | bytes 20971520 | tf_op jit(solution)/shard_map/reduce_scatter | solution.py:32
  73.1 4.1 copy-start.4
  77.2 12.3 %copy-start.3 = (bf16[128,256]{1,0:T(8,128)(2,1)S(1)}, bf16[128,256]{1,0:T(8,128)(2,1)}, u32[]{:S(2)}) copy-start(bf16[128,256]{1,0:T(8,128)(2,1)} %param.7) | copy-start | bytes 196612
  91.0 408.9 %reduce-scatter.5.cloned.1.call-start = ((), (), s32[]{:S(2)}) async-start(), calls=%async_computation.4 | async-start | bytes 4325376 | tf_op jit(solution)/shard_map/reduce_scatter | solution.py:39
  501.0 4.3 copy-start.2
  505.3 109.1 %all-to-all-start = ((bf16[128,128,256]{2,1,0:T(8,128)(2,1)}), bf16[128,128,256]{2,1,0:T(8,128)(2,1)}, u32[]{:S(2)}, u32[]{:S(2)}) async-start(bf16[128,128,256]{2,1,0:T(8,128)(2,1)} %stack.2), calls=%async_computation.2 | async-start | bytes 16777216 | tf_op jit(solution)/shard_map/all_to_all | solution.py:12
  513.7 186.2 %all-reduce.6.cloned.1.call-start = ((), (), s32[]{:S(2)}) async-start(), calls=%async_computation.5 | async-start | bytes 6291456 | tf_op jit(solution)/shard_map/psum | solution.py:47
  700.0 46.9 %copy-start.1 = (bf16[1,1536,256]{2,1,0:T(8,128)(2,1)S(1)}, bf16[1,1536,256]{2,1,0:T(8,128)(2,1)}, u32[]{:S(2)}) copy-start(bf16[1,1536,256]{2,1,0:T(8,128)(2,1)} %param.6) | copy-start | bytes 2359300
Sparse Core Ops, SparseCore 0:
  91.2 148.1 reduce-scatter.2
  423.1 76.8 reduce-scatter.4
  627.2 72.7 all-reduce.5
